TPU v7x, 128 devices: a whole 4x4x4 slice. The times are simulated.
128 devices in a mesh: row: 16 (over x, y), col: 8 (over z, core).
Axes of the slice: x: 4, y: 4, z: 4, core: 2. Of those that a mesh axis runs over, the one named last changes fastest.
Arguments:
- diag_tile: float32 [256, 256], replicated, may hold values from 0 to 10, as said below
- panel_block: float32 [24576, 256], P(('row', 'col')), may hold values from -3 to 3
- trailing: bfloat16 [24576, 24576], P('row', 'col'), may hold values from -6 to 6
- vec_head: float32 [512, 256], P('col'), may hold values from -6 to 6
- vec_rest: float32 [512, 24576], P('col', 'row'), may hold values from -6 to 6
Outputs:
- panel: float32 [24576, 256], P(('row', 'col'))
- trailing_new: bfloat16 [24576, 24576], P('row', 'col')
- whitened: float32 [512, 256], P('col')
- vec_new: float32 [512, 24576], P('col', 'row')
Inputs may be any that keep to these rules, and one draw needn't show every extreme that they name: `diag_tile`: symmetric positive definite.
All inputs are finite; a program needn't handle non-finite values.
Results may differ from a plain program's by a relative error of at most 0.0054.
Values may be sent and summed in bfloat16 or wider, within the bound.
A program may use at most 128 MiB of HBM per device.

v0:
```python
import jax
import jax.numpy as jnp
from jax import lax
from jax.sharding import PartitionSpec as P


def right_solve(factor, rhs):
    return lax.linalg.triangular_solve(factor, rhs, left_side=False, lower=True, transpose_a=True)


def per_device(diag_tile, panel_block, trailing, vec_head, vec_rest):
    factor = jnp.linalg.cholesky(diag_tile)
    panel = right_solve(factor, panel_block)
    panel_half = panel.astype(jnp.bfloat16)
    row_panel = lax.all_gather(panel_half, "col", axis=0, tiled=True)
    complete = lax.all_gather(row_panel, "row", axis=0, tiled=True)
    width = trailing.shape[1]
    col_panel = lax.dynamic_slice_in_dim(complete, lax.axis_index("col") * width, width, 0)
    update = lax.dot_general(
        row_panel, col_panel, (((1,), (1,)), ((), ())), preferred_element_type=jnp.float32
    )
    trailing_new = (trailing.astype(jnp.float32) - update).astype(jnp.bfloat16)
    whitened = right_solve(factor, vec_head)
    whitened_half = whitened.astype(jnp.bfloat16)
    product = lax.dot_general(
        whitened_half, row_panel, (((1,), (1,)), ((), ())), preferred_element_type=jnp.float32
    )
    vec_new = vec_rest - product
    return (panel, trailing_new, whitened, vec_new)


def solution(mesh):
    in_specs = (P(), P(("row", "col"), None), P("row", "col"), P("col", None), P("col", "row"))
    out_specs = (P(("row", "col"), None), P("row", "col"), P("col", None), P("col", "row"))
    return jax.shard_map(
        per_device, mesh=mesh, in_specs=in_specs, out_specs=out_specs, check_vma=False
    )
```

profile of v0, /device:TPU:0, one launch (start us, length us, event | category | flops | bytes accessed | tf_op | source)
XLA Modules:
  0.0 196.7 jit_solution(699865556386835207)
XLA Ops:
  7.2 1.1 copy.9
  8.3 1.0 fusion.1
  9.3 11.7 %cholesky.50 = f32[128,128]{1,0:T(8,128)S(1)} custom-call(f32[128,128]{1,0:T(8,128)S(1)} %cholesky.118), custom_call_target="Cholesky" | custom-call | tf_op jit(solution)/shard_map/jit(cholesky)/cholesky | solution.py:12
  21.1 9.8 %custom-call.16 = f32[1,128,128]{1,2,0:T(8,128)S(1)} custom-call(f32[1,128,128]{2,1,0:T(8,128)S(1)} %get-tuple-element.27), custom_call_target="InvertDiagBlocksLowerTriangular" | custom-call | tf_op jit(solution)/shard_map/jit(cholesky)/cholesky | solution.py:12
  30.9 0.2 constant_dynamic-update-slice_fusion
  31.1 0.3 convolution_subtract_fusion.2
  31.4 11.7 %cholesky.105 = f32[128,128]{1,0:T(8,128)S(1)} custom-call(f32[128,128]{1,0:T(8,128)S(1)} %convolution_subtract_fusion.2), custom_call_target="Cholesky" | custom-call | tf_op jit(solution)/shard_map/jit(cholesky)/cholesky | solution.py:12
  43.1 0.6 compare_reduce_fusion
  45.2 4.1 %while.1 = (s32[]{:T(128)}, f32[256,256]{1,0:T(8,128)S(1)}, s32[2,2]{1,0:T(2,128)S(1)}, f32[2,128,128]{2,1,0:T(8,128)S(1)}, s32[]{:T(128)}) while((s32[]{:T(128)}, f32[256,256]{1,0:T(8,128)S(1)}, s32[2,2]{1,0:T(2,128)S(1)}, f32[2,128,128]{2,1,0:T(8,128)S(1)}, s32[]{:T(128)}) %tuple.28), condition=%wide.while_cond, body=%wide.while_body.sunk | while | flops 2 | bytes 131189 | solution.py:8
  45.3 0.6 fusion.26
  45.9 1.4 bitcast_dynamic-update-slice_fusion.2
  47.3 0.6 fusion.26
  47.9 1.4 bitcast_dynamic-update-slice_fusion.2
  49.3 19.7 %custom-call.17 = f32[2,128,128]{1,2,0:T(8,128)S(1)} custom-call(f32[2,128,128]{2,1,0:T(8,128)S(1)} %get-tuple-element.11), custom_call_target="InvertDiagBlocksLowerTriangular" | custom-call | tf_op jit(solution)/shard_map/triangular_solve | solution.py:8
  69.0 1.1 fusion.2
  70.1 1.2 convolution_subtract_fusion.1
  71.3 0.2 fusion.9
  71.6 0.7 fusion.15
  72.3 15.8 %all_gather.6 = bf16[1536,256]{1,0:T(8,128)(2,1)} all-gather(bf16[192,256]{1,0:T(8,128)(2,1)S(1)} %get-tuple-element.20), channel_id=1, replica_groups=mesh['row'=16,'col'=8] {'col'}, dimensions={0}, use_global_device_ids=true | all-gather | bytes 884736 | tf_op jit(solution)/shard_map/all_gather | solution.py:15
  88.1 0.9 fusion.7
  89.0 1.0 convolution_subtract_fusion.3
  90.2 2.4 %convolution_subtract_fusion = f32[64,1536]{1,0:T(8,128)} fusion(f32[64,1536]{1,0:T(8,128)} %param.9, bf16[1536,256]{1,0:T(8,128)(2,1)} %all_gather.6, f32[64,256]{1,0:T(8,128)S(1)} %pad_maximum_fusion.1), kind=kOutput, calls=%fused_computation.3 | convolution fusion | flops 50446336 | bytes 1638400 | tf_op jit(solution)/shard_map/dot_general | solution.py:25
  92.6 86.4 %all-gather.2.cloned.1.call-done = bf16[24576,256]{1,0:T(8,128)(2,1)} async-done(((bf16[1536,256]{1,0:T(8,128)(2,1)}), bf16[24576,256]{1,0:T(8,128)(2,1)}) %all-gather.2.cloned.1.call-update) | async-done | bytes 12582928 | tf_op jit(solution)/shard_map/all_gather | solution.py:16
  179.0 10.8 %subtract_convert_fusion = bf16[1536,3072]{1,0:T(8,128)(2,1)} fusion(bf16[1536,3072]{1,0:T(8,128)(2,1)} %param.7, bf16[1536,256]{1,0:T(8,128)(2,1)} %all_gather.6, bf16[24576,256]{1,0:T(8,128)(2,1)} %all-gather.2.cloned.1.call-done, s32[]{:T(128)S(6)} %select_n.8), kind=kOutput, calls=%fused_computation.2 | convolution fusion | flops 2430074880 | bytes 21233668 | tf_op jit(solution)/shard_map/dot_general | solution.py:19
  (16 shorter events, 0.5 us)
Async XLA Ops:
  7.2 171.9 %all-gather.2.cloned.1.call-start = ((), (), s32[]{:S(2)}) async-start(), calls=%async_computation | async-start | bytes 13369344 | tf_op jit(solution)/shard_map/all_gather | solution.py:16
  90.2 99.6 %copy-start = (f32[64,256]{1,0:T(8,128)}, f32[64,256]{1,0:T(8,128)S(1)}, u32[]{:S(2)}) copy-start(f32[64,256]{1,0:T(8,128)S(1)} %pad_maximum_fusion.1) | copy-start | bytes 196612
Sparse Core Ops, SparseCore 0:
  88.2 90.8 all-gather.1
where the time goes:
time: 198 us; the launch traced here: 197 us
  waiting for transfers between devices  86.4 us (44%)
  other arithmetic  55.4 us (28%)
  matrix products  18.3 us (9%)
  blocking collectives  15.8 us (8%)
  between operations  15.5 us (8%)
  local copies, waits for them, and re-layouts  5.13 us (3%)
    all_gather x1, waiting for transfers between devices, per_device(): complete = lax.all_gather(row_panel, 'row', axis=0, tiled=True)  86.4 us
    another operation x6, other arithmetic, per_device(): factor = jnp.linalg.cholesky(diag_tile)  34 us
    another operation x4, other arithmetic, right_solve(): lax.linalg.triangular_solve(factor, rhs, left_side=False, lower=True, tra...  19.7 us
    all_gather x1, blocking collectives, per_device(): row_panel = lax.all_gather(panel_half, 'col', axis=0, tiled=True)  15.8 us
    dot_general x1, matrix products, per_device(): lax.dot_general(row_panel, col_panel, (((1,), (1,)), ((), ())), preferred...  10.8 us
    another operation x6, matrix products, right_solve(): lax.linalg.triangular_solve(factor, rhs, left_side=False, lower=True, tra...  4.65 us
  transfers between devices with their start and end apart: 1, of which 1 were waited for; matrix products, arithmetic and copies ran while one was open for 2% of the time, Pallas kernels for 0%

commit v1 on v0

v1 whole, which is shorter than its diff:
```python
import jax
import jax.numpy as jnp
from jax import lax
from jax.experimental import pallas as pl
from jax.experimental.pallas import tpu as pltpu
from jax.sharding import PartitionSpec as P

f32, bf16 = jnp.float32, jnp.bfloat16
MESH = pl.DeviceIdType.MESH
BK = 16
NB = 256
RB = 192
MIB = 1 << 20


def split3(x):
    h = x.astype(bf16)
    r = x - h.astype(f32)
    m = r.astype(bf16)
    return h, m, (r - m.astype(f32)).astype(bf16)


def dot(a, b):
    return lax.dot_general(a, b, (((1,), (0,)), ((), ())), preferred_element_type=f32)


def dot_nt(a, b):
    return lax.dot_general(a, b, (((1,), (1,)), ((), ())), preferred_element_type=f32)


def block_step(k, m_ref, w_ref, g_ref, rhs_ref):
    t, o = divmod(k, 128)
    lane = lax.broadcasted_iota(jnp.int32, (8, 128), 1)
    rows, S = [], []
    for i in range(BK):
        parts = [
            jnp.broadcast_to(m_ref[k + i : k + i + 1, c * 128 : c * 128 + 128], (8, 128)) for c in range(2)
        ]
        S.append([jnp.broadcast_to(parts[t][:, o + j : o + j + 1], (8, 128)) for j in range(i + 1)])
        eye = jnp.where(lane == o + i, 1.0, 0.0)
        parts[t] = jnp.where((lane >= o) & (lane < o + BK), eye, parts[t])
        rows.append(parts)
    inv, F = [], [[None] * BK for _ in range(BK)]
    for j in range(BK):
        inv.append(1.0 / S[j][j])
        for i in range(j + 1, BK):
            F[i][j] = S[i][j] * inv[j]
            for n in range(j + 1, i + 1):
                S[i][n] = S[i][n] - F[i][j] * S[n][j]
            rows[i] = [rows[i][c] - F[i][j] * rows[j][c] for c in range(2)]
    for i in range(BK):
        rs = lax.rsqrt(S[i][i])
        for c in range(2):
            v = rows[i][c] * rs
            if c == t:
                v = jnp.where(lane < o + BK, v, 0.0)
            elif c > t:
                v = jnp.zeros_like(v)
            w_ref[k + i : k + i + 1, c * 128 : c * 128 + 128] = v[0:1]
    if k + BK >= NB:
        return
    g = [None] * BK
    for i in reversed(range(BK)):
        acc = [rows[i][c] * inv[i] for c in range(2)]
        for j in range(i + 1, BK):
            acc = [acc[c] - F[j][i] * g[j][c] for c in range(2)]
        g[i] = acc
        for c in range(2):
            g_ref[i : i + 1, c * 128 : c * 128 + 128] = acc[c][0:1]
    gh, gm, gl = split3(g_ref[...])
    for q, (a, b) in enumerate(((gh, gh), (gm, gm), (gl, gh))):
        rhs_ref[q, o : o + BK, :] = a
        rhs_ref[q, 128 + o : 128 + o + BK, :] = b
    n0 = k + BK
    h, m, l = split3(m_ref[n0:NB, t * 128 : t * 128 + 128])
    hm = jnp.concatenate([h, m], 1)
    up = dot(hm, rhs_ref[0]) + dot(hm, rhs_ref[1])
    up = up + dot(jnp.concatenate([h, l], 1), rhs_ref[2])
    lanes = lax.broadcasted_iota(jnp.int32, (NB - n0, NB), 1)
    old = jnp.where((lanes >= k) & (lanes < k + BK), 0.0, m_ref[n0:NB, :])
    m_ref[n0:NB, :] = old - up
    zero = jnp.zeros((BK, NB), bf16)
    for q in range(3):
        rhs_ref[q, o : o + BK, :] = zero
        rhs_ref[q, 128 + o : 128 + o + BK, :] = zero


def factor_kernel(a_ref, b_ref, v_ref, panel_ref, white_ref, xh_ref, wh_ref, m_ref, w_ref, g_ref, rhs_ref):
    m_ref[...] = a_ref[...]
    rhs_ref[...] = jnp.zeros_like(rhs_ref)
    for k in range(0, NB, BK):
        block_step(k, m_ref, w_ref, g_ref, rhs_ref)
    wh, wm, _ = split3(w_ref[...])

    def solve(x):
        h, m, _ = split3(x)
        return dot_nt(h, wh) + (dot_nt(h, wm) + dot_nt(m, wh))

    x = solve(b_ref[...])
    panel_ref[...] = x
    half = x.astype(bf16)
    xh_ref[0] = half[:, 0:128]
    xh_ref[1] = half[:, 128:256]
    v = solve(v_ref[...])
    white_ref[...] = v
    wh_ref[...] = v.astype(bf16)


class Torus:
    def __init__(self):
        row, col = lax.axis_index("row"), lax.axis_index("col")
        self.x, self.y = row // 4, row % 4
        self.z, self.c = col // 2, col % 2

    def at(self, x=None, y=None, z=None, c=None):
        x = self.x if x is None else x
        y = self.y if y is None else y
        z = self.z if z is None else z
        c = self.c if c is None else c
        return {"row": x * 4 + y, "col": z * 2 + c}

    def step(self, dim, by):
        return self.at(**{dim: (getattr(self, dim) + by) % 4})

    def held(self, hx, hy):
        same = jnp.where(hy // 2 == self.c, 1, 0)
        yy = jnp.where(same == 1, hy, 3 - hy)
        return (yy % 2) * 8 + 2 * hx + (1 - same)


def comm_kernel(x_ref, row_ref, col_ref, send, recv, local):
    me = Torus()
    barrier = pltpu.get_barrier_semaphore()
    same = jnp.where(me.y // 2 == me.c, 1, 0)
    src = (me.z, jnp.where(same == 1, me.y, 3 - me.y), me.x, 1 - same)
    dst = (me.z, jnp.where(me.c == 0, me.y, 3 - me.y), me.x, me.y // 2)
    own = (dst[0] == me.x) & (dst[1] == me.y) & (dst[2] == me.z) & (dst[3] == me.c)
    away = jnp.logical_not(own)
    for dim in ("x", "y", "z"):
        for by in (1, -1):
            pl.semaphore_signal(barrier, inc=1, device_id=me.step(dim, by), device_id_type=MESH)
    pl.semaphore_signal(barrier, inc=1, device_id=me.at(c=1 - me.c), device_id_type=MESH)

    @pl.when(away)
    def _():
        pl.semaphore_signal(barrier, inc=1, device_id=me.at(*src), device_id_type=MESH)
        pl.semaphore_wait(barrier, 8)

    @pl.when(own)
    def _():
        pl.semaphore_wait(barrier, 7)

    started = []

    def copy(a, b, idx, to):
        return pltpu.make_async_remote_copy(
            src_ref=a, dst_ref=b, send_sem=send.at[idx], recv_sem=recv.at[idx], device_id=to, device_id_type=MESH
        )

    def go(a, b, idx, to):
        d = copy(a, b, idx, to)
        d.start()
        started.append(d)

    def rows_of(ref, block, lo, n):
        return ref.at[:, pl.ds(pl.multiple_of(block * RB + lo, 16), n), :]

    def wait(ref, idx):
        copy(ref, ref, idx, me.at(c=1 - me.c)).wait_recv()

    first = me.at(*dst)
    mine = (me.y % 2) * 8 + 2 * me.z + me.c
    hold = me.held(me.x, me.y)
    sc = copy(x_ref, rows_of(col_ref, mine, 0, RB), 0, first)

    @pl.when(away)
    def _():
        sc.start()

    @pl.when(own)
    def _():
        pltpu.make_async_copy(x_ref, rows_of(col_ref, hold, 0, RB), recv.at[0]).start()

    zb = lambda d, core=None: 2 * ((me.z + d) % 4) + (me.c if core is None else core)
    sib = me.at(c=1 - me.c)
    keep = pltpu.make_async_copy(x_ref, rows_of(row_ref, zb(0), 0, RB), local)
    keep.start()
    go(x_ref, rows_of(row_ref, zb(0), 0, RB), 1, me.step("z", 1))
    go(x_ref, rows_of(row_ref, zb(0), 0, RB), 2, me.step("z", -1))
    go(x_ref, rows_of(row_ref, zb(0), 0, RB), 5, sib)

    H, Q = RB // 2, RB // 4
    parts = ((0, "x", "y", 9), (H, "y", "x", 29))

    def chunk(part, a, b, lo=0, n=H):
        base, d1, d2, _ = part
        p = (getattr(me, d1) + a) % 4
        q = (getattr(me, d2) + b) % 4
        hx, hy = (p, q) if d1 == "x" else (q, p)
        return rows_of(col_ref, me.held(hx, hy), base + lo, n)

    REL = (0, -1, 1, 2)

    def send2(part, rel, lo=0, n=H):
        _, d1, d2, sem = part
        ref = chunk(part, REL[rel], 0, lo, n)
        go(ref, ref, sem + 4 + 4 * rel + 0, me.step(d2, 1))
        go(ref, ref, sem + 4 + 4 * rel + 1, me.step(d2, -1))

    def forward(part, dim, sem, ref_lo, ref_hi, which):
        if which == 0:
            go(ref_lo, ref_lo, sem + 2, me.step(dim, 1))
        else:
            go(ref_hi, ref_hi, sem + 3, me.step(dim, -1))

    def dim1(part, which):
        _, d1, d2, sem = part
        a = (-1, 1)[which]
        wait(chunk(part, a, 0), sem + which)
        forward(part, d1, sem, chunk(part, a, 0, 0, Q), chunk(part, a, 0, Q, Q), which)
        send2(part, 1 + which)

    def dim2(part, rel, which):
        _, d1, d2, sem = part
        b = (-1, 1)[which]
        s = sem + 4 + 4 * rel
        wait(chunk(part, REL[rel], b), s + which)
        forward(part, d2, s, chunk(part, REL[rel], b, 0, Q), chunk(part, REL[rel], b, Q, Q), which)

    def far1(part):
        sem = part[3]
        wait(chunk(part, 2, 0, 0, Q), sem + 2)
        wait(chunk(part, 2, 0, Q, Q), sem + 3)
        send2(part, 3)

    def far2(part, rel):
        s = part[3] + 4 + 4 * rel
        wait(chunk(part, REL[rel], 2, 0, Q), s + 2)
        wait(chunk(part, REL[rel], 2, Q, Q), s + 3)

    wait(rows_of(col_ref, hold, 0, RB), 0)
    for part in parts:
        ref, sem = chunk(part, 0, 0), part[3]
        go(ref, ref, sem + 0, me.step(part[1], 1))
        go(ref, ref, sem + 1, me.step(part[1], -1))
    for part in parts:
        send2(part, 0)
    for w in range(2):
        d = (-1, 1)[w]
        blk = zb(d)
        wait(rows_of(row_ref, blk, 0, RB), 1 + w)
        half = rows_of(row_ref, blk, w * H, H)
        go(half, half, 3 + w, me.step("z", (1, -1)[w]))
        whole = rows_of(row_ref, blk, 0, RB)
        go(whole, whole, 6 + w, sib)
    for w in range(2):
        for part in parts:
            dim1(part, w)
    for w in range(2):
        for part in parts:
            dim2(part, 0, w)
    for part in parts:
        far1(part)
    for w in range(2):
        wait(rows_of(row_ref, zb(2), w * H, H), 3 + w)
    whole = rows_of(row_ref, zb(2), 0, RB)
    go(whole, whole, 8, sib)
    for rel in (1, 2, 3):
        for w in range(2):
            for part in parts:
                dim2(part, rel, w)
    for rel in range(4):
        for part in parts:
            far2(part, rel)
    for i, d in enumerate((0, -1, 1, 2)):
        wait(rows_of(row_ref, zb(d, 1 - me.c), 0, RB), 5 + i)
    keep.wait()
    for d in started:
        d.wait_send()

    @pl.when(away)
    def _():
        sc.wait_send()


def update_kernel(row_ref, col_ref, t_ref, wh_ref, v_ref, out_ref, vec_ref):
    i, j = pl.program_id(0), pl.program_id(1)
    tm, tn = out_ref.shape
    r = jnp.concatenate([row_ref[0, pl.ds(i * tm, tm), :], row_ref[1, pl.ds(i * tm, tm), :]], 1)
    c = jnp.concatenate([col_ref[0, pl.ds(j * tn, tn), :], col_ref[1, pl.ds(j * tn, tn), :]], 1)
    out_ref[...] = (t_ref[...].astype(f32) - dot_nt(r, c)).astype(bf16)

    @pl.when((i == 0) & (j == 0))
    def _():
        full = jnp.concatenate([row_ref[0], row_ref[1]], 1)
        vec_ref[...] = v_ref[...] - dot_nt(wh_ref[...], full)


VM = pl.BlockSpec(memory_space=pltpu.VMEM)


def per_device(diag_tile, panel_block, trailing, vec_head, vec_rest):
    nv = vec_head.shape[0]
    mr, mc = trailing.shape
    panel, white, xh, wh = pl.pallas_call(
        factor_kernel,
        out_shape=(
            jax.ShapeDtypeStruct((RB, NB), f32),
            jax.ShapeDtypeStruct((nv, NB), f32),
            jax.ShapeDtypeStruct((2, RB, 128), bf16),
            jax.ShapeDtypeStruct((nv, NB), bf16),
        ),
        in_specs=[VM] * 3,
        out_specs=(VM,) * 4,
        scratch_shapes=[
            pltpu.VMEM((NB, NB), f32),
            pltpu.VMEM((NB, NB), f32),
            pltpu.VMEM((BK, NB), f32),
            pltpu.VMEM((3, NB, NB), bf16),
        ],
        compiler_params=pltpu.CompilerParams(vmem_limit_bytes=12 * MIB),
        cost_estimate=pl.CostEstimate(flops=12 * 10**9, bytes_accessed=0, transcendentals=0),
        name="factor",
    )(diag_tile, panel_block, vec_head)
    rowp, colp = pl.pallas_call(
        comm_kernel,
        out_shape=(jax.ShapeDtypeStruct((2, mr, 128), bf16), jax.ShapeDtypeStruct((2, mc, 128), bf16)),
        in_specs=[VM],
        out_specs=(VM,) * 2,
        scratch_shapes=[
            pltpu.SemaphoreType.DMA((49,)),
            pltpu.SemaphoreType.DMA((49,)),
            pltpu.SemaphoreType.DMA,
        ],
        compiler_params=pltpu.CompilerParams(
            collective_id=0, has_side_effects=True, vmem_limit_bytes=12 * MIB
        ),
        cost_estimate=pl.CostEstimate(flops=10 * 10**9, bytes_accessed=0, transcendentals=0),
        name="share",
    )(xh)
    tm, tn = 512, 1024
    out, vec = pl.pallas_call(
        update_kernel,
        grid=(mr // tm, mc // tn),
        out_shape=(jax.ShapeDtypeStruct((mr, mc), bf16), jax.ShapeDtypeStruct((nv, mr), f32)),
        in_specs=[
            VM,
            VM,
            pl.BlockSpec((tm, tn), lambda i, j: (i, j)),
            VM,
            VM,
        ],
        out_specs=(pl.BlockSpec((tm, tn), lambda i, j: (i, j)), pl.BlockSpec((nv, mr), lambda i, j: (0, 0))),
        compiler_params=pltpu.CompilerParams(vmem_limit_bytes=40 * MIB),
        name="update",
    )(rowp, colp, trailing, wh, vec_rest)
    return (panel, out, white, vec)


def solution(mesh):
    in_specs = (P(), P(("row", "col"), None), P("row", "col"), P("col", None), P("col", "row"))
    out_specs = (P(("row", "col"), None), P("row", "col"), P("col", None), P("col", "row"))
    return jax.shard_map(per_device, mesh=mesh, in_specs=in_specs, out_specs=out_specs, check_vma=False)
```

time: 198 us -> 56 us (0.28)
  waiting for transfers between devices: 86.4 us -> 0 us
  other arithmetic: 55.4 us -> 0.01 us
  Pallas kernels: 0 us -> 52.4 us
  matrix products: 18.3 us -> 0 us
  blocking collectives: 15.8 us -> 0 us
  between operations: 15.5 us -> 0.69 us
  local copies, waits for them, and re-layouts: 5.13 us -> 2.72 us
    all_gather x1 -> x0, waiting for transfers between devices: 86.4 us -> none  [per_device(): complete = lax.all_gather(row_panel, 'row', axis=0, tiled=True)]
    another operation x10 -> x0, other arithmetic: 53.7 us -> none  [the longest x6 34 us: per_device(): factor = jnp.linalg.cholesky(diag_tile)]
    pallas_call x0 -> x3, Pallas kernels: none -> 52.4 us  [the longest x1 31.2 us: per_device(): pl.pallas_call(comm_kernel, out_shape=(jax.ShapeDtypeStruct((2, mr, 128),...]
    all_gather x1 -> x0, blocking collectives: 15.8 us -> none  [per_device(): row_panel = lax.all_gather(panel_half, 'col', axis=0, tiled=True)]
    dot_general x2 -> x0, matrix products: 13.2 us -> none  [the longest x1 10.8 us: per_device(): lax.dot_general(row_panel, col_panel, (((1,), (1,)), ((), ())), preferred...]
    another operation x8 -> x0, matrix products: 5.12 us -> none  [the longest x6 4.65 us: right_solve(): lax.linalg.triangular_solve(factor, rhs, left_side=False, lower=True, tra...]
    another operation x9 -> x0, local copies, waits for them, and re-layouts: 4.05 us -> none
  transfers between devices with their start and end apart: 1 -> 0, of which waited for: 1 -> 0; matrix products, arithmetic and copies ran while one was open for 2% -> 0% of each run, Pallas kernels for 0% -> 0%
where the time goes in v1:
time: 56 us; the launch traced here: 55.8 us
  Pallas kernels  52.4 us (94%)
  local copies, waits for them, and re-layouts  2.72 us (5%)
  between operations  0.69 us (1%)
    pallas_call x1, Pallas kernels, per_device(): pl.pallas_call(comm_kernel, out_shape=(jax.ShapeDtypeStruct((2, mr, 128),...  31.2 us
    pallas_call x1, Pallas kernels, per_device(): pl.pallas_call(factor_kernel, out_shape=(jax.ShapeDtypeStruct((RB, NB), f...  13.1 us
    pallas_call x1, Pallas kernels, per_device(): pl.pallas_call(update_kernel, grid=(mr // tm, mc // tn), out_shape=(jax.S...  8.05 us
    unnamed x14, local copies, waits for them, and re-layouts  2.72 us

profile of v1, /device:TPU:0, one launch (start us, length us, event | category | flops | bytes accessed | tf_op | source)
XLA Modules:
  0.0 55.8 jit_solution(1614097824903620598)
XLA Ops:
  0.6 0.0 copy-start.1
  0.6 0.9 %copy-done.1 = f32[256,256]{1,0:T(8,128)S(1)} copy-done((f32[256,256]{1,0:T(8,128)S(1)}, f32[256,256]{1,0:T(8,128)}, u32[]{:S(2)}) %copy-start.1) | copy-done | bytes 262168
  1.6 0.0 copy-start.2
  1.6 0.9 %copy-done.2 = f32[192,256]{1,0:T(8,128)S(1)} copy-done((f32[192,256]{1,0:T(8,128)S(1)}, f32[192,256]{1,0:T(8,128)}, u32[]{:S(2)}) %copy-start.2) | copy-done | bytes 196632
  2.5 0.0 copy-start.3
  2.5 0.8 %copy-done.3 = f32[64,256]{1,0:T(8,128)S(1)} copy-done((f32[64,256]{1,0:T(8,128)S(1)}, f32[64,256]{1,0:T(8,128)}, u32[]{:S(2)}) %copy-start.3) | copy-done | bytes 65560
  3.3 0.0 slice-start
  3.4 0.0 slice-start.1
  3.4 13.1 %factor.1 = (f32[192,256]{1,0:T(8,128)}, f32[64,256]{1,0:T(8,128)}, bf16[2,192,128]{2,1,0:T(8,128)(2,1)S(1)}, bf16[64,256]{1,0:T(8,128)(2,1)S(1)}) custom-call(f32[256,256]{1,0:T(8,128)S(1)} %copy-done.1, f32[192,256]{1,0:T(8,128)S(1)} %copy-done.2, f32[64,256]{1,0:T(8,128)S(1)} %copy-done.3), custom_call_target="tpu_custom_call" | custom-call | flops 12000000000 | tf_op jit(solution)/shard_map/factor/pallas_call | solution.py:305
  16.4 0.0 slice-start.2
  16.4 0.0 copy-start
  16.4 31.2 %share.1 = (bf16[2,1536,128]{2,1,0:T(8,128)(2,1)S(1)}, bf16[2,3072,128]{2,1,0:T(8,128)(2,1)S(1)}) custom-call(bf16[2,192,128]{2,1,0:T(8,128)(2,1)S(1)} %get-tuple-element.13.x_ref), custom_call_target="tpu_custom_call" | custom-call | flops 10000000000 | tf_op jit(solution)/shard_map/share/pallas_call | solution.py:325
  47.7 0.0 slice-done
  47.7 0.0 slice-done.1
  47.7 0.0 slice-done.2
  47.7 0.0 copy-done
  47.7 8.0 %update.1 = (bf16[1536,3072]{1,0:T(8,128)(2,1)}, f32[64,1536]{1,0:T(8,128)}) custom-call(bf16[2,1536,128]{2,1,0:T(8,128)(2,1)S(1)} %get-tuple-element.14.row_ref, bf16[2,3072,128]{2,1,0:T(8,128)(2,1)S(1)} %get-tuple-element.15.col_ref, bf16[1536,3072]{1,0:T(8,128)(2,1)S(1)} %bitcast.1, bf16[64,256]{1,0:T(8,128)(2,1)S(1)} %get-tuple-element.16.wh_ref, ...), custom_call_target="tpu_custom_call" | custom-call | tf_op jit(solution)/shard_map/update/pallas_call | solution.py:342
  (1 shorter events, 0.0 us)
Async XLA Ops:
  0.6 1.0 %copy-start.1 = (f32[256,256]{1,0:T(8,128)S(1)}, f32[256,256]{1,0:T(8,128)}, u32[]{:S(2)}) copy-start(f32[256,256]{1,0:T(8,128)} %a_ref.1) | copy-start | bytes 786436
  1.6 0.9 %copy-start.2 = (f32[192,256]{1,0:T(8,128)S(1)}, f32[192,256]{1,0:T(8,128)}, u32[]{:S(2)}) copy-start(f32[192,256]{1,0:T(8,128)} %b_ref.1) | copy-start | bytes 589828
  2.5 0.8 %copy-start.3 = (f32[64,256]{1,0:T(8,128)S(1)}, f32[64,256]{1,0:T(8,128)}, u32[]{:S(2)}) copy-start(f32[64,256]{1,0:T(8,128)} %v_ref.2) | copy-start | bytes 196612
  3.3 44.3 %slice-start = ((s8[9437184]{0:T(1024)(128)(4,1)}), s8[4194304]{0:T(1024)(128)(4,1)S(1)}, s32[]{:S(2)}) async-start(s8[9437184]{0:T(1024)(128)(4,1)} %bitcast), calls=%async_computation | async-start | bytes 8388608
  3.4 44.4 %slice-start.1 = ((s8[9437184]{0:T(1024)(128)(4,1)}), s8[4194304]{0:T(1024)(128)(4,1)S(1)}, s32[]{:S(2)}) async-start(s8[9437184]{0:T(1024)(128)(4,1)} %bitcast), calls=%async_computation.1 | async-start | bytes 8388608
  16.4 31.3 %slice-start.2 = ((s8[9437184]{0:T(1024)(128)(4,1)}), s8[1048576]{0:T(1024)(128)(4,1)S(1)}, s32[]{:S(2)}) async-start(s8[9437184]{0:T(1024)(128)(4,1)} %bitcast), calls=%async_computation.2 | async-start | bytes 2097152
  16.4 31.3 %copy-start = (f32[64,1536]{1,0:T(8,128)S(1)}, f32[64,1536]{1,0:T(8,128)}, u32[]{:S(2)}) copy-start(f32[64,1536]{1,0:T(8,128)} %v_ref.3) | copy-start | bytes 1179652

commit v2 on v0

v2 whole, which is shorter than its diff:
```python
import jax
import jax.numpy as jnp
from jax import lax
from jax.experimental import pallas as pl
from jax.experimental.pallas import tpu as pltpu
from jax.sharding import PartitionSpec as P

f32, bf16 = jnp.float32, jnp.bfloat16
MESH = pl.DeviceIdType.MESH
BK = 16
NB = 256
RB = 192
MIB = 1 << 20


def split3(x):
    h = x.astype(bf16)
    r = x - h.astype(f32)
    m = r.astype(bf16)
    return h, m, (r - m.astype(f32)).astype(bf16)


def dot(a, b):
    return lax.dot_general(a, b, (((1,), (0,)), ((), ())), preferred_element_type=f32)


def dot_nt(a, b):
    return lax.dot_general(a, b, (((1,), (1,)), ((), ())), preferred_element_type=f32)


def block_step(k, m_ref, w_ref, g_ref, rhs_ref):
    t, o = divmod(k, 128)
    lane = lax.broadcasted_iota(jnp.int32, (1, 8, 128), 2)
    nth = lax.broadcasted_iota(jnp.int32, (BK, 8, 128), 0)
    R = [
        jnp.stack([jnp.broadcast_to(m_ref[k + i : k + i + 1, c * 128 : c * 128 + 128], (8, 128)) for i in range(BK)])
        for c in range(2)
    ]
    S = [jnp.broadcast_to(R[t][j:, :, o + j : o + j + 1], (BK - j, 8, 128)) for j in range(BK)]
    R[t] = jnp.where((lane >= o) & (lane < o + BK), jnp.where(lane - o == nth, 1.0, 0.0), R[t])
    inv, F, out = [], [], [[], []]
    for j in range(BK):
        inv.append(1.0 / S[j][0:1])
        for c in range(2):
            out[c].append(R[c][0:1])
        if j == BK - 1:
            break
        f = S[j][1:] * inv[j]
        for n in range(j + 1, BK):
            S[n] = S[n] - f[n - j - 1 :] * S[j][n - j : n - j + 1]
        R = [R[c][1:] - f * R[c][0:1] for c in range(2)]
        F.append(f)
    piv = jnp.concatenate([S[j][0:1] for j in range(BK)], 0)
    rs = lax.rsqrt(piv)
    U = [jnp.concatenate(out[c], 0) for c in range(2)]
    for c in range(2):
        v = U[c] * rs
        if c == t:
            v = jnp.where(lane < o + BK, v, 0.0)
        elif c > t:
            v = jnp.zeros_like(v)
        for i in range(BK):
            w_ref[k + i : k + i + 1, c * 128 : c * 128 + 128] = v[i, 0:1]
    if k + BK >= NB:
        return
    iv = jnp.concatenate(inv, 0)
    Z = [U[c] * iv for c in range(2)]
    for i in reversed(range(BK)):
        for c in range(2):
            g_ref[i : i + 1, c * 128 : c * 128 + 128] = Z[c][i, 0:1]
        if i:
            f = jnp.concatenate([F[n][i - n - 1 : i - n] for n in range(i)], 0)
            Z = [Z[c][:i] - f * Z[c][i : i + 1] for c in range(2)]
    gh, gm, gl = split3(g_ref[...])
    for q, (a, b) in enumerate(((gh, gh), (gm, gm), (gl, gh))):
        rhs_ref[q, o : o + BK, :] = a
        rhs_ref[q, 128 + o : 128 + o + BK, :] = b
    n0 = k + BK
    h, m, l = split3(m_ref[n0:NB, t * 128 : t * 128 + 128])
    hm = jnp.concatenate([h, m], 1)
    up = dot(hm, rhs_ref[0]) + dot(hm, rhs_ref[1])
    up = up + dot(jnp.concatenate([h, l], 1), rhs_ref[2])
    lanes = lax.broadcasted_iota(jnp.int32, (NB - n0, NB), 1)
    old = jnp.where((lanes >= k) & (lanes < k + BK), 0.0, m_ref[n0:NB, :])
    m_ref[n0:NB, :] = old - up
    zero = jnp.zeros((BK, NB), bf16)
    for q in range(3):
        rhs_ref[q, o : o + BK, :] = zero
        rhs_ref[q, 128 + o : 128 + o + BK, :] = zero


class Torus:
    def __init__(self):
        row, col = lax.axis_index("row"), lax.axis_index("col")
        self.x, self.y = row // 4, row % 4
        self.z, self.c = col // 2, col % 2

    def at(self, x=None, y=None, z=None, c=None):
        x = self.x if x is None else x
        y = self.y if y is None else y
        z = self.z if z is None else z
        c = self.c if c is None else c
        return {"row": x * 4 + y, "col": z * 2 + c}

    def step(self, dim, by):
        return self.at(**{dim: (getattr(self, dim) + by) % 4})


NSEM = 22


class Share:
    def __init__(self, me, half, x_ref, row_ref, col_ref, send, recv):
        self.me, self.half = me, half
        self.x, self.row, self.col = x_ref.at[half], row_ref.at[half], col_ref.at[half]
        self.send, self.recv = send.at[half], recv.at[half]
        self.started = []

    def copy(self, a, b, sem, to, arrive=None):
        return pltpu.make_async_remote_copy(
            src_ref=a,
            dst_ref=b,
            send_sem=self.send.at[sem],
            recv_sem=self.recv.at[sem if arrive is None else arrive],
            device_id=to,
            device_id_type=MESH,
        )

    def origin(self, y):
        same = jnp.where(y // 2 == self.me.c, 1, 0)
        return jnp.where(same == 1, y, 3 - y) % 2, 1 - same

    def scatter(self):
        me = self.me
        yh = jnp.where(me.c == 0, me.y, 3 - me.y)
        for part in range(2):
            src = self.x.at[part]
            dst = self.col.at[me.y % 2, me.z, me.c, part]
            arrive = part
            for d in range(4):
                if part == 0:
                    to = me.at((me.x + d) % 4, yh, me.x, me.y // 2)
                else:
                    to = me.at(me.z, (me.y + d) % 4, me.x, me.y // 2)
                cp = self.copy(src, dst, 4 * part + d, to, arrive)
                if d == 0:
                    mine = me.own[part]

                    @pl.when(jnp.logical_not(mine))
                    def _():
                        cp.start()

                    @pl.when(mine)
                    def _():
                        pltpu.make_async_copy(src, dst, self.recv.at[arrive]).start()
                else:
                    cp.start()
                self.started.append((cp, me.own[part] if d == 0 else None))

    def rows(self):
        me = self.me
        dst = self.row.at[2 * me.z + me.c]
        i = 0
        for d in range(4):
            for e in range(2):
                if d == 0 and e == 0:
                    continue
                cp = self.copy(self.x, dst, 8 + i, me.at(z=(me.z + d) % 4, c=(me.c + e) % 2))
                cp.start()
                self.started.append((cp, None))
                i += 1
        self.keep = pltpu.make_async_copy(self.x, dst, self.send.at[21])
        self.keep.start()

    def held(self, part, at):
        if part == 0:
            yy, cc = self.origin(at)
            return self.col.at[yy, :, cc, 0]
        return self.col.at[:, at, :, 1]

    def relay(self):
        me = self.me
        for part in range(2):
            dim = "yx"[part]
            ref = self.held(part, getattr(me, dim))
            self.copy(ref, ref, part, me.step(dim, 1), part).wait_recv()
            for d in range(1, 4):
                cp = self.copy(ref, ref, 15 + 3 * part + d - 1, me.step(dim, d))
                cp.start()
                self.started.append((cp, None))

    def finish(self):
        me = self.me
        i = 0
        for d in range(4):
            for e in range(2):
                if d == 0 and e == 0:
                    continue
                dst = self.row.at[2 * ((me.z + 4 - d) % 4) + (me.c + e) % 2]
                self.copy(dst, dst, 8 + i, me.step("z", 1)).wait_recv()
                i += 1
        self.keep.wait()
        for part in range(2):
            dim = "yx"[part]
            for d in range(1, 4):
                ref = self.held(part, (getattr(me, dim) + 4 - d) % 4)
                self.copy(ref, ref, 15 + 3 * part + d - 1, me.step(dim, 1)).wait_recv()
        for cp, unless in self.started:
            if unless is None:
                cp.wait_send()
            else:

                @pl.when(jnp.logical_not(unless))
                def _():
                    cp.wait_send()


def greet(me):
    barrier = pltpu.get_barrier_semaphore()

    def tell(to):
        pl.semaphore_signal(barrier, inc=1, device_id=to, device_id_type=MESH)

    same = jnp.where(me.y // 2 == me.c, 1, 0)
    fy = jnp.where(same == 1, me.y, 3 - me.y)
    me.own = (
        (me.x == me.z) & (me.y // 2 == me.c) & (me.c == 0),
        (me.x == me.z) & (me.y // 2 == me.c),
    )
    for d in range(4):
        to = me.at(me.z, fy, (me.z + d) % 4, 1 - same)
        if d == 0:
            pl.when(jnp.logical_not(me.own[0]))(lambda: tell(to))
        else:
            tell(to)
    for d in range(4):
        to = me.at(me.z, 2 * me.c + (me.y + d // 2) % 2, me.x, (me.c + d) % 2)
        if d == 0:
            pl.when(jnp.logical_not(me.own[1]))(lambda: tell(to))
        else:
            tell(to)
    for d in range(4):
        for e in range(2):
            if d or e:
                tell(me.at(z=(me.z + d) % 4, c=(me.c + e) % 2))
    for dim in "xy":
        for d in range(1, 4):
            tell(me.step(dim, d))
    return barrier, 21 - jnp.where(me.own[0], 1, 0) - jnp.where(me.own[1], 1, 0)


def panel_kernel(
    a_hbm, b_hbm, v_hbm, panel_ref, white_ref, wh_ref, row_ref, col_ref,
    m_ref, w_ref, g_ref, rhs_ref, bv_ref, x_ref, send, recv, local,
):
    loads = [
        pltpu.make_async_copy(a_hbm, m_ref, local.at[0]),
        pltpu.make_async_copy(b_hbm, bv_ref.at[0:RB], local.at[1]),
        pltpu.make_async_copy(v_hbm, bv_ref.at[RB:NB], local.at[2]),
    ]
    for cp in loads:
        cp.start()
    me = Torus()
    barrier, count = greet(me)
    rhs_ref[...] = jnp.zeros_like(rhs_ref)
    shares = [Share(me, h, x_ref, row_ref, col_ref, send, recv) for h in range(2)]
    loads[0].wait()
    for k in range(0, NB, BK):
        block_step(k, m_ref, w_ref, g_ref, rhs_ref)
        if k == RELAY_AFTER:
            shares[0].relay()
        if k + BK in (128, 256):
            half = k // 128
            n = k + BK
            if half == 0:
                loads[1].wait()
                loads[2].wait()
            wh, wm, _ = split3(w_ref[half * 128 : n, 0:n])
            bh, bm, _ = split3(bv_ref[:, 0:n])
            x = dot_nt(bh, wh) + (dot_nt(bh, wm) + dot_nt(bm, wh))
            xb = x.astype(bf16)
            for part in range(2):
                x_ref[half, part] = xb[part * 96 : part * 96 + 96]
            panel_ref[:, half * 128 : n] = x[0:RB]
            white_ref[:, half * 128 : n] = x[RB:NB]
            wh_ref[:, half * 128 : n] = xb[RB:NB]
            if half == 0:
                pl.semaphore_wait(barrier, count)
            shares[half].scatter()
            shares[half].rows()
    shares[1].relay()
    for s in shares:
        s.finish()


def update_kernel(row_ref, col_ref, t_ref, wh_ref, v_ref, p_in, w_in, out_ref, vec_ref, p_ref, w_ref):
    i = pl.program_id(0)
    tm = out_ref.shape[0]
    rs = pl.ds(pl.multiple_of(i * tm, tm), tm)
    r = jnp.concatenate([row_ref[0, rs, :], row_ref[1, rs, :]], 1)
    c = jnp.concatenate([col_ref[0], col_ref[1]], 1)
    out_ref[...] = (t_ref[rs, :].astype(f32) - dot_nt(r, c)).astype(bf16)

    @pl.when(i == 0)
    def _():
        full = jnp.concatenate([row_ref[0], row_ref[1]], 1)
        vec_ref[...] = v_ref[...] - dot_nt(wh_ref[...], full)
        p_ref[...] = p_in[...]
        w_ref[...] = w_in[...]


VM = pl.BlockSpec(memory_space=pltpu.VMEM)
HB = pl.BlockSpec(memory_space=pltpu.MemorySpace.HBM)
RELAY_AFTER = 13 * BK


def per_device(diag_tile, panel_block, trailing, vec_head, vec_rest):
    nv = vec_head.shape[0]
    mr, mc = trailing.shape
    panel, white, wh, rowp, colp = pl.pallas_call(
        panel_kernel,
        out_shape=(
            jax.ShapeDtypeStruct((RB, NB), f32),
            jax.ShapeDtypeStruct((nv, NB), f32),
            jax.ShapeDtypeStruct((nv, NB), bf16),
            jax.ShapeDtypeStruct((2, 8, 2, 96, 128), bf16),
            jax.ShapeDtypeStruct((2, 2, 4, 2, 2, 96, 128), bf16),
        ),
        in_specs=[HB] * 3,
        out_specs=(VM,) * 5,
        scratch_shapes=[
            pltpu.VMEM((NB, NB), f32),
            pltpu.VMEM((NB, NB), f32),
            pltpu.VMEM((BK, NB), f32),
            pltpu.VMEM((3, NB, NB), bf16),
            pltpu.VMEM((NB, NB), f32),
            pltpu.VMEM((2, 2, 96, 128), bf16),
            pltpu.SemaphoreType.DMA((2, NSEM)),
            pltpu.SemaphoreType.DMA((2, NSEM)),
            pltpu.SemaphoreType.DMA((3,)),
        ],
        compiler_params=pltpu.CompilerParams(
            collective_id=0, has_side_effects=True, vmem_limit_bytes=12 * MIB
        ),
        cost_estimate=pl.CostEstimate(flops=20 * 10**9, bytes_accessed=0, transcendentals=0),
        name="panel",
    )(diag_tile, panel_block, vec_head)
    rowp = rowp.reshape(2, mr, 128)
    colp = colp.reshape(2, mc, 128)
    tm = 384
    whole = lambda shape: pl.BlockSpec(shape, lambda i: (0, 0))
    out, vec, panel, white = pl.pallas_call(
        update_kernel,
        grid=(mr // tm,),
        out_shape=(
            jax.ShapeDtypeStruct((mr, mc), bf16),
            jax.ShapeDtypeStruct((nv, mr), f32),
            jax.ShapeDtypeStruct((RB, NB), f32),
            jax.ShapeDtypeStruct((nv, NB), f32),
        ),
        in_specs=[VM] * 7,
        out_specs=(
            pl.BlockSpec((tm, mc), lambda i: (i, 0)),
            whole((nv, mr)),
            whole((RB, NB)),
            whole((nv, NB)),
        ),
        compiler_params=pltpu.CompilerParams(vmem_limit_bytes=40 * MIB),
        name="update",
    )(rowp, colp, trailing, wh, vec_rest, panel, white)
    return (panel, out, white, vec)


def solution(mesh):
    in_specs = (P(), P(("row", "col"), None), P("row", "col"), P("col", None), P("col", "row"))
    out_specs = (P(("row", "col"), None), P("row", "col"), P("col", None), P("col", "row"))
    return jax.shard_map(per_device, mesh=mesh, in_specs=in_specs, out_specs=out_specs, check_vma=False)
```

time: 198 us -> 50.5 us (0.26)
  waiting for transfers between devices: 86.4 us -> 0 us
  other arithmetic: 55.4 us -> 0 us
  Pallas kernels: 0 us -> 45.2 us
  matrix products: 18.3 us -> 0 us
  blocking collectives: 15.8 us -> 0 us
  between operations: 15.5 us -> 0.68 us
    all_gather x1 -> x0, waiting for transfers between devices: 86.4 us -> none  [per_device(): complete = lax.all_gather(row_panel, 'row', axis=0, tiled=True)]
    another operation x10 -> x0, other arithmetic: 53.7 us -> none  [the longest x6 34 us: per_device(): factor = jnp.linalg.cholesky(diag_tile)]
    pallas_call x0 -> x2, Pallas kernels: none -> 45.2 us  [the longest x1 39.4 us: per_device(): pl.pallas_call(panel_kernel, out_shape=(jax.ShapeDtypeStruct((RB, NB), f3...]
    all_gather x1 -> x0, blocking collectives: 15.8 us -> none  [per_device(): row_panel = lax.all_gather(panel_half, 'col', axis=0, tiled=True)]
    dot_general x2 -> x0, matrix products: 13.2 us -> none  [the longest x1 10.8 us: per_device(): lax.dot_general(row_panel, col_panel, (((1,), (1,)), ((), ())), preferred...]
    another operation x8 -> x0, matrix products: 5.12 us -> none  [the longest x6 4.65 us: right_solve(): lax.linalg.triangular_solve(factor, rhs, left_side=False, lower=True, tra...]
    another operation x9 -> x0, local copies, waits for them, and re-layouts: 4.05 us -> none
    unnamed x3 -> x10, local copies, waits for them, and re-layouts: 1.09 us -> 3.75 us
  transfers between devices with their start and end apart: 1 -> 0, of which waited for: 1 -> 0; matrix products, arithmetic and copies ran while one was open for 2% -> 0% of each run, Pallas kernels for 0% -> 0%
where the time goes in v2:
time: 50.5 us; the launch traced here: 49.6 us
  Pallas kernels  45.2 us (90%)
  local copies, waits for them, and re-layouts  3.75 us (7%)
  between operations  0.68 us (1%)
    pallas_call x1, Pallas kernels, per_device(): pl.pallas_call(panel_kernel, out_shape=(jax.ShapeDtypeStruct((RB, NB), f3...  39.4 us
    pallas_call x1, Pallas kernels, per_device(): pl.pallas_call(update_kernel, grid=(mr // tm,), out_shape=(jax.ShapeDtype...  5.78 us
    unnamed x10, local copies, waits for them, and re-layouts  3.75 us

profile of v2, /device:TPU:0, one launch (start us, length us, event | category | flops | bytes accessed | tf_op | source)
XLA Modules:
  0.0 49.6 jit_solution(17464575589200056274)
XLA Ops:
  0.6 0.0 copy-start.1
  0.6 0.0 copy-start
  0.7 0.0 copy-start.2
  0.7 1.1 %copy-done.2 = f32[256,256]{1,0:T(8,128)S(1)} copy-done((f32[256,256]{1,0:T(8,128)S(1)}, f32[256,256]{1,0:T(8,128)}, u32[]{:S(2)}) %copy-start.2) | copy-done | bytes 262168
  1.8 0.0 copy-start.3
  1.8 1.5 %copy-done.3 = f32[192,256]{1,0:T(8,128)S(1)} copy-done((f32[192,256]{1,0:T(8,128)S(1)}, f32[192,256]{1,0:T(8,128)}, u32[]{:S(2)}) %copy-start.3) | copy-done | bytes 196632
  3.2 0.0 copy-start.4
  3.2 1.2 %copy-done.4 = f32[64,256]{1,0:T(8,128)S(1)} copy-done((f32[64,256]{1,0:T(8,128)S(1)}, f32[64,256]{1,0:T(8,128)}, u32[]{:S(2)}) %copy-start.4) | copy-done | bytes 65560
  4.4 39.4 %panel.1 = (f32[192,256]{1,0:T(8,128)S(1)}, f32[64,256]{1,0:T(8,128)S(1)}, bf16[64,256]{1,0:T(8,128)(2,1)S(1)}, bf16[2,8,2,96,128]{4,3,2,1,0:T(8,128)(2,1)S(1)}, bf16[2,2,4,2,2,96,128]{6,5,4,3,2,1,0:T(8,128)(2,1)S(1)}) custom-call(f32[256,256]{1,0:T(8,128)S(1)} %copy-done.2, f32[192,256]{1,0:T(8,128)S(1)} %copy-done.3, f32[64,256]{1,0:T(8,128)S(1)} %copy-done.4), custom_call_target="tpu_custom_call" | custom-call | flops 20000000000 | tf_op jit(solution)/shard_map/panel/pallas_call | solution.py:320
  43.8 0.0 copy-done.1
  43.8 0.0 copy-done
  43.8 5.8 %update.1 = (bf16[1536,3072]{1,0:T(8,128)(2,1)}, f32[64,1536]{1,0:T(8,128)}, f32[192,256]{1,0:T(8,128)}, f32[64,256]{1,0:T(8,128)}) custom-call(bf16[2,1536,128]{2,1,0:T(8,128)(2,1)S(1)} %bitcast.3, bf16[2,3072,128]{2,1,0:T(8,128)(2,1)S(1)} %bitcast.2, bf16[1536,3072]{1,0:T(8,128)(2,1)S(1)} %copy-done, bf16[64,256]{1,0:T(8,128)(2,1)S(1)} %get-tuple-element.15.wh_ref, ...), custom_call_target="tpu_custom_call" | custom-call | tf_op jit(solution)/shard_map/update/pallas_call | solution.py:352
Async XLA Ops:
  0.6 43.2 %copy-start.1 = (f32[64,1536]{1,0:T(8,128)S(1)}, f32[64,1536]{1,0:T(8,128)}, u32[]{:S(2)}) copy-start(f32[64,1536]{1,0:T(8,128)} %v_ref.1) | copy-start | bytes 1179652
  0.6 43.2 %copy-start = (bf16[1536,3072]{1,0:T(8,128)(2,1)S(1)}, bf16[1536,3072]{1,0:T(8,128)(2,1)}, u32[]{:S(2)}) copy-start(bf16[1536,3072]{1,0:T(8,128)(2,1)} %t_ref.1) | copy-start | bytes 28311556
  0.7 1.1 %copy-start.2 = (f32[256,256]{1,0:T(8,128)S(1)}, f32[256,256]{1,0:T(8,128)}, u32[]{:S(2)}) copy-start(f32[256,256]{1,0:T(8,128)} %a_hbm.1) | copy-start | bytes 786436
  1.8 1.5 %copy-start.3 = (f32[192,256]{1,0:T(8,128)S(1)}, f32[192,256]{1,0:T(8,128)}, u32[]{:S(2)}) copy-start(f32[192,256]{1,0:T(8,128)} %b_hbm.1) | copy-start | bytes 589828
  3.2 1.2 %copy-start.4 = (f32[64,256]{1,0:T(8,128)S(1)}, f32[64,256]{1,0:T(8,128)}, u32[]{:S(2)}) copy-start(f32[64,256]{1,0:T(8,128)} %v_hbm.1) | copy-start | bytes 196612

commit v3 on v2

v3 whole, which is shorter than its diff:
```python
import jax
import jax.numpy as jnp
from jax import lax
from jax.experimental import pallas as pl
from jax.experimental.pallas import tpu as pltpu
from jax.sharding import PartitionSpec as P

f32, bf16 = jnp.float32, jnp.bfloat16
MESH = pl.DeviceIdType.MESH
BK = 16
NB = 256
RB = 192
MIB = 1 << 20


def split3(x):
    h = x.astype(bf16)
    r = x - h.astype(f32)
    m = r.astype(bf16)
    return h, m, (r - m.astype(f32)).astype(bf16)


def dot(a, b):
    return lax.dot_general(a, b, (((1,), (0,)), ((), ())), preferred_element_type=f32)


def dot_nt(a, b):
    return lax.dot_general(a, b, (((1,), (1,)), ((), ())), preferred_element_type=f32)


def block_step(k, m_ref, w_ref, g_ref, rhs_ref):
    t, o = divmod(k, 128)
    lane = lax.broadcasted_iota(jnp.int32, (1, 8, 128), 2)
    nth = lax.broadcasted_iota(jnp.int32, (BK, 8, 128), 0)
    R = [
        jnp.stack([jnp.broadcast_to(m_ref[k + i : k + i + 1, c * 128 : c * 128 + 128], (8, 128)) for i in range(BK)])
        for c in range(2)
    ]
    S = [jnp.broadcast_to(R[t][j:, :, o + j : o + j + 1], (BK - j, 8, 128)) for j in range(BK)]
    R[t] = jnp.where((lane >= o) & (lane < o + BK), jnp.where(lane - o == nth, 1.0, 0.0), R[t])
    inv, F, out = [], [], [[], []]
    for j in range(BK):
        inv.append(1.0 / S[j][0:1])
        for c in range(2):
            out[c].append(R[c][0:1])
        if j == BK - 1:
            break
        f = S[j][1:] * inv[j]
        for n in range(j + 1, BK):
            S[n] = S[n] - f[n - j - 1 :] * S[j][n - j : n - j + 1]
        R = [R[c][1:] - f * R[c][0:1] for c in range(2)]
        F.append(f)
    piv = jnp.concatenate([S[j][0:1] for j in range(BK)], 0)
    rs = lax.rsqrt(piv)
    U = [jnp.concatenate(out[c], 0) for c in range(2)]
    for c in range(2):
        v = U[c] * rs
        if c == t:
            v = jnp.where(lane < o + BK, v, 0.0)
        elif c > t:
            v = jnp.zeros_like(v)
        for i in range(BK):
            w_ref[k + i : k + i + 1, c * 128 : c * 128 + 128] = v[i, 0:1]
    if k + BK >= NB:
        return
    iv = jnp.concatenate(inv, 0)
    Z = [U[c] * iv for c in range(2)]
    for i in reversed(range(BK)):
        for c in range(2):
            g_ref[i : i + 1, c * 128 : c * 128 + 128] = Z[c][i, 0:1]
        if i:
            f = jnp.concatenate([F[n][i - n - 1 : i - n] for n in range(i)], 0)
            Z = [Z[c][:i] - f * Z[c][i : i + 1] for c in range(2)]
    gh, gm, gl = split3(g_ref[...])
    for q, (a, b) in enumerate(((gh, gh), (gm, gm), (gl, gh))):
        rhs_ref[q, o : o + BK, :] = a
        rhs_ref[q, 128 + o : 128 + o + BK, :] = b
    n0 = k + BK
    h, m, l = split3(m_ref[n0:NB, t * 128 : t * 128 + 128])
    hm = jnp.concatenate([h, m], 1)
    up = dot(hm, rhs_ref[0]) + dot(hm, rhs_ref[1])
    up = up + dot(jnp.concatenate([h, l], 1), rhs_ref[2])
    lanes = lax.broadcasted_iota(jnp.int32, (NB - n0, NB), 1)
    old = jnp.where((lanes >= k) & (lanes < k + BK), 0.0, m_ref[n0:NB, :])
    m_ref[n0:NB, :] = old - up
    zero = jnp.zeros((BK, NB), bf16)
    for q in range(3):
        rhs_ref[q, o : o + BK, :] = zero
        rhs_ref[q, 128 + o : 128 + o + BK, :] = zero


class Torus:
    def __init__(self):
        row, col = lax.axis_index("row"), lax.axis_index("col")
        self.x, self.y = row // 4, row % 4
        self.z, self.c = col // 2, col % 2

    def at(self, x=None, y=None, z=None, c=None):
        x = self.x if x is None else x
        y = self.y if y is None else y
        z = self.z if z is None else z
        c = self.c if c is None else c
        return {"row": x * 4 + y, "col": z * 2 + c}

    def step(self, dim, by):
        return self.at(**{dim: (getattr(self, dim) + by) % 4})

    def origin(self, y):
        same = jnp.where(y // 2 == self.c, 1, 0)
        return jnp.where(same == 1, y, 3 - y) % 2, 1 - same


NSEM = 37


class Share:
    def __init__(self, me, half, row_ref, col_ref, send, recv):
        self.me = me
        self.row, self.col = row_ref.at[half], col_ref.at[half]
        self.send, self.recv = send.at[half], recv.at[half]
        self.started = []

    def copy(self, ref, sem, to):
        return pltpu.make_async_remote_copy(
            src_ref=ref,
            dst_ref=ref,
            send_sem=self.send.at[sem],
            recv_sem=self.recv.at[sem],
            device_id=to,
            device_id_type=MESH,
        )

    def go(self, ref, sem, to):
        cp = self.copy(ref, sem, to)
        cp.start()
        self.started.append(cp)

    def wait(self, ref, sem):
        self.copy(ref, sem, self.me.step("x", 1)).wait_recv()

    def chunk(self, part, e=0, d=0):
        me = self.me
        back = (e, d) if part == 0 else (d, e)
        hx, hy = (me.x + 4 - back[0]) % 4, (me.y + 4 - back[1]) % 4
        yy, cc = me.origin(hy)
        return self.col.at[yy, hx, cc, part]

    def rowblock(self, d=0, e=0):
        me = self.me
        return self.row.at[2 * ((me.z + 4 - d) % 4) + (me.c + e) % 2]

    def second(self, part, e):
        for d in range(1, 4):
            self.go(self.chunk(part, e), 6 + 12 * part + 3 * e + d - 1, self.me.step("yx"[part], d))

    def begin(self):
        for part in range(2):
            for d in range(1, 4):
                self.go(self.chunk(part), 3 * part + d - 1, self.me.step("xy"[part], d))
        for part in range(2):
            self.second(part, 0)

    def others(self):
        return [(d, e) for d in range(4) for e in range(2) if d or e]

    def rows(self):
        me = self.me
        for i, (d, e) in enumerate(self.others()):
            self.go(self.rowblock(), 30 + i, me.at(z=(me.z + d) % 4, c=(me.c + e) % 2))

    def relay(self):
        for e in (1, 3, 2):
            for part in range(2):
                self.wait(self.chunk(part, e), 3 * part + e - 1)
                self.second(part, e)

    def finish(self):
        for i, (d, e) in enumerate(self.others()):
            self.wait(self.rowblock(d, e), 30 + i)
        for e in (0, 1, 3, 2):
            for part in range(2):
                for d in range(1, 4):
                    self.wait(self.chunk(part, e, d), 6 + 12 * part + 3 * e + d - 1)
        for cp in self.started:
            cp.wait_send()


def greet(me):
    barrier = pltpu.get_barrier_semaphore()

    def tell(to):
        pl.semaphore_signal(barrier, inc=1, device_id=to, device_id_type=MESH)

    same = jnp.where(me.y // 2 == me.c, 1, 0)
    me.own = (me.x == me.z) & (me.y // 2 == me.c) & (me.c == 0)
    me.other = jnp.logical_not(me.own)
    source = me.at(me.z, jnp.where(same == 1, me.y, 3 - me.y), me.x, 1 - same)
    pl.when(me.other)(lambda: tell(source))
    for d in range(4):
        for e in range(2):
            if d or e:
                tell(me.at(z=(me.z + d) % 4, c=(me.c + e) % 2))
    for dim in "xy":
        for d in range(1, 4):
            tell(me.step(dim, d))
    return barrier, 14 - jnp.where(me.own, 1, 0)


def panel_kernel(
    a_hbm, b_hbm, v_hbm, t_hbm, r_hbm, panel_ref, white_ref, wh_ref, row_ref, col_ref, t_ref, r_ref,
    m_ref, w_ref, g_ref, rhs_ref, bv_ref, held_ref, send, recv, first, local,
):
    loads = [
        pltpu.make_async_copy(a_hbm, m_ref, local.at[0]),
        pltpu.make_async_copy(b_hbm, bv_ref.at[0:RB], local.at[1]),
        pltpu.make_async_copy(v_hbm, bv_ref.at[RB:NB], local.at[2]),
    ]
    for cp in loads:
        cp.start()
    me = Torus()
    barrier, count = greet(me)
    rhs_ref[...] = jnp.zeros_like(rhs_ref)
    shares = [Share(me, h, row_ref, col_ref, send, recv) for h in range(2)]
    holder = me.at(me.z, jnp.where(me.c == 0, me.y, 3 - me.y), me.x, me.y // 2)
    raw = []
    for h in range(2):
        src = b_hbm.at[:, h * 128 : h * 128 + 128]
        raw.append(
            pltpu.make_async_remote_copy(
                src_ref=src,
                dst_ref=held_ref.at[h],
                send_sem=first.at[2 + h],
                recv_sem=first.at[h],
                device_id=holder,
                device_id_type=MESH,
            )
        )
    loads[0].wait()
    later = [pltpu.make_async_copy(t_hbm, t_ref, local.at[3]), pltpu.make_async_copy(r_hbm, r_ref, local.at[4])]
    for cp in later:
        cp.start()

    def solve(b, w):
        n = b.shape[1]
        bh, bm, _ = split3(b)
        wh, wm, _ = split3(w)
        return dot_nt(bh, wh) + (dot_nt(bh, wm) + dot_nt(bm, wh))

    def part_of(half):
        c0, n = half * 128, half * 128 + 128
        w = w_ref[c0:n, 0:n]
        raw[half].wait_recv()
        if half == 0:
            b = held_ref[0]
        else:
            b = jnp.concatenate([held_ref[0], held_ref[1]], 1)
        xb = solve(b, w).astype(bf16)
        for part in range(2):
            shares[half].chunk(part)[...] = xb[part * 96 : part * 96 + 96]
        if half == 0:
            loads[1].wait()
            loads[2].wait()
        x = solve(bv_ref[:, 0:n], w)
        xb = x.astype(bf16)
        for part in range(2):
            row_ref[half, 2 * me.z + me.c, part] = xb[part * 96 : part * 96 + 96]
        shares[half].begin()
        panel_ref[:, c0:n] = x[0:RB]
        white_ref[:, c0:n] = x[RB:NB]
        wh_ref[:, c0:n] = xb[RB:NB]
        shares[half].rows()

    for i in range(NB // BK):
        block_step(i * BK, m_ref, w_ref, g_ref, rhs_ref)
        if i == 0:
            pl.semaphore_wait(barrier, count)

            @pl.when(me.other)
            def _():
                for cp in raw:
                    cp.start()

            @pl.when(me.own)
            def _():
                for h in range(2):
                    pltpu.make_async_copy(b_hbm.at[:, h * 128 : h * 128 + 128], held_ref.at[h], first.at[h]).start()

        if i == SEND_AFTER:
            part_of(0)
        if i == RELAY_AFTER:
            shares[0].relay()
    part_of(1)
    shares[1].relay()
    for s in shares:
        s.finish()

    @pl.when(me.other)
    def _():
        for cp in raw:
            cp.wait_send()

    for cp in later:
        cp.wait()


def update_kernel(row_ref, col_ref, t_ref, wh_ref, v_ref, p_in, w_in, out_ref, vec_ref, p_ref, w_ref):
    i = pl.program_id(0)
    tm = out_ref.shape[0]
    rs = pl.ds(pl.multiple_of(i * tm, tm), tm)
    r = jnp.concatenate([row_ref[0, rs, :], row_ref[1, rs, :]], 1)
    c = jnp.concatenate([col_ref[0], col_ref[1]], 1)
    out_ref[...] = (t_ref[rs, :].astype(f32) - dot_nt(r, c)).astype(bf16)

    @pl.when(i == 0)
    def _():
        full = jnp.concatenate([row_ref[0], row_ref[1]], 1)
        vec_ref[...] = v_ref[...] - dot_nt(wh_ref[...], full)
        p_ref[...] = p_in[...]
        w_ref[...] = w_in[...]


VM = pl.BlockSpec(memory_space=pltpu.VMEM)
HB = pl.BlockSpec(memory_space=pltpu.MemorySpace.HBM)
SEND_AFTER, RELAY_AFTER = 9, 14


def per_device(diag_tile, panel_block, trailing, vec_head, vec_rest):
    nv = vec_head.shape[0]
    mr, mc = trailing.shape
    inputs = [
        pltpu.with_memory_space_constraint(a, pltpu.MemorySpace.HBM)
        for a in (diag_tile, panel_block, vec_head, trailing, vec_rest)
    ]
    panel, white, wh, rowp, colp, tiles, rest = pl.pallas_call(
        panel_kernel,
        out_shape=(
            jax.ShapeDtypeStruct((RB, NB), f32),
            jax.ShapeDtypeStruct((nv, NB), f32),
            jax.ShapeDtypeStruct((nv, NB), bf16),
            jax.ShapeDtypeStruct((2, 8, 2, 96, 128), bf16),
            jax.ShapeDtypeStruct((2, 2, 4, 2, 2, 96, 128), bf16),
            jax.ShapeDtypeStruct((mr, mc), bf16),
            jax.ShapeDtypeStruct((nv, mr), f32),
        ),
        in_specs=[HB] * 5,
        out_specs=(VM,) * 7,
        scratch_shapes=[
            pltpu.VMEM((NB, NB), f32),
            pltpu.VMEM((NB, NB), f32),
            pltpu.VMEM((BK, NB), f32),
            pltpu.VMEM((3, NB, NB), bf16),
            pltpu.VMEM((NB, NB), f32),
            pltpu.VMEM((2, RB, 128), f32),
            pltpu.SemaphoreType.DMA((2, NSEM)),
            pltpu.SemaphoreType.DMA((2, NSEM)),
            pltpu.SemaphoreType.DMA((4,)),
            pltpu.SemaphoreType.DMA((5,)),
        ],
        compiler_params=pltpu.CompilerParams(
            collective_id=0, has_side_effects=True, vmem_limit_bytes=12 * MIB
        ),
        cost_estimate=pl.CostEstimate(flops=20 * 10**9, bytes_accessed=0, transcendentals=0),
        name="panel",
    )(*inputs)
    rowp = rowp.reshape(2, mr, 128)
    colp = colp.reshape(2, mc, 128)
    tm = 384
    whole = lambda shape: pl.BlockSpec(shape, lambda i: (0, 0))
    out, vec, panel, white = pl.pallas_call(
        update_kernel,
        grid=(mr // tm,),
        out_shape=(
            jax.ShapeDtypeStruct((mr, mc), bf16),
            jax.ShapeDtypeStruct((nv, mr), f32),
            jax.ShapeDtypeStruct((RB, NB), f32),
            jax.ShapeDtypeStruct((nv, NB), f32),
        ),
        in_specs=[VM] * 7,
        out_specs=(
            pl.BlockSpec((tm, mc), lambda i: (i, 0)),
            whole((nv, mr)),
            whole((RB, NB)),
            whole((nv, NB)),
        ),
        compiler_params=pltpu.CompilerParams(vmem_limit_bytes=40 * MIB),
        name="update",
    )(rowp, colp, tiles, wh, rest, panel, white)
    return (panel, out, white, vec)


def solution(mesh):
    in_specs = (P(), P(("row", "col"), None), P("row", "col"), P("col", None), P("col", "row"))
    out_specs = (P(("row", "col"), None), P("row", "col"), P("col", None), P("col", "row"))
    return jax.shard_map(per_device, mesh=mesh, in_specs=in_specs, out_specs=out_specs, check_vma=False)
```

time: 50.5 us -> 42.4 us (0.84)
  Pallas kernels: 45.2 us -> 41.3 us
  local copies, waits for them, and re-layouts: 3.75 us -> 0 us
    pallas_call x1, Pallas kernels: 39.4 us -> 35.5 us  [per_device(): pl.pallas_call(panel_kernel, out_shape=(jax.ShapeDtypeStruct((RB, NB), f3...]
    unnamed x10 -> x0, local copies, waits for them, and re-layouts: 3.75 us -> none
where the time goes in v3:
time: 42.4 us; the launch traced here: 41.9 us
  Pallas kernels  41.3 us (97%)
  between operations  0.64 us (2%)
    pallas_call x1, Pallas kernels, per_device(): pl.pallas_call(panel_kernel, out_shape=(jax.ShapeDtypeStruct((RB, NB), f3...  35.5 us
    pallas_call x1, Pallas kernels, per_device(): pl.pallas_call(update_kernel, grid=(mr // tm,), out_shape=(jax.ShapeDtype...  5.78 us

profile of v3, /device:TPU:0, one launch (start us, length us, event | category | flops | bytes accessed | tf_op | source)
XLA Modules:
  0.0 41.9 jit_solution(4463098843137793575)
XLA Ops:
  0.6 35.5 %panel.1 = (f32[192,256]{1,0:T(8,128)S(1)}, f32[64,256]{1,0:T(8,128)S(1)}, bf16[64,256]{1,0:T(8,128)(2,1)S(1)}, bf16[2,8,2,96,128]{4,3,2,1,0:T(8,128)(2,1)S(1)},...) custom-call(f32[256,256]{1,0:T(8,128)} %a_hbm.1, ...), custom_call_target="tpu_custom_call" | custom-call | flops 20000000000 | tf_op jit(solution)/shard_map/panel/pallas_call | solution.py:334
  36.1 5.8 %update.1 = (bf16[1536,3072]{1,0:T(8,128)(2,1)}, f32[64,1536]{1,0:T(8,128)}, f32[192,256]{1,0:T(8,128)}, f32[64,256]{1,0:T(8,128)}) custom-call(bf16[2,1536,128]{2,1,0:T(8,128)(2,1)S(1)} %bitcast.3, bf16[2,3072,128]{2,1,0:T(8,128)(2,1)S(1)} %bitcast.2, bf16[1536,3072]{1,0:T(8,128)(2,1)S(1)} %get-tuple-element.17.t_ref, ...), custom_call_target="tpu_custom_call" | custom-call | tf_op jit(solution)/shard_map/update/pallas_call | solution.py:369

commit v4 on v3

--- a/solution.py
+++ b/solution.py
@@ -31,62 +31,54 @@
 def block_step(k, m_ref, w_ref, g_ref, rhs_ref):
     t, o = divmod(k, 128)
     lane = lax.broadcasted_iota(jnp.int32, (1, 8, 128), 2)
+    tile = lax.broadcasted_iota(jnp.int32, (1, 8, 128), 1) // 4
     nth = lax.broadcasted_iota(jnp.int32, (BK, 8, 128), 0)
-    R = [
+    T = [
         jnp.stack([jnp.broadcast_to(m_ref[k + i : k + i + 1, c * 128 : c * 128 + 128], (8, 128)) for i in range(BK)])
         for c in range(2)
     ]
-    S = [jnp.broadcast_to(R[t][j:, :, o + j : o + j + 1], (BK - j, 8, 128)) for j in range(BK)]
-    R[t] = jnp.where((lane >= o) & (lane < o + BK), jnp.where(lane - o == nth, 1.0, 0.0), R[t])
-    inv, F, out = [], [], [[], []]
+    S = [jnp.broadcast_to(T[t][j:, :, o + j : o + j + 1], (BK - j, 8, 128)) for j in range(BK)]
+    R = jnp.where(tile == 0, T[0], T[1])
+    at = lane + 128 * tile - k
+    R = jnp.where((at >= 0) & (at < BK), jnp.where(at == nth, 1.0, 0.0), R)
+    inv, F, out = [], [], []
     for j in range(BK):
         inv.append(1.0 / S[j][0:1])
-        for c in range(2):
-            out[c].append(R[c][0:1])
+        out.append(R[0:1])
         if j == BK - 1:
             break
         f = S[j][1:] * inv[j]
         for n in range(j + 1, BK):
             S[n] = S[n] - f[n - j - 1 :] * S[j][n - j : n - j + 1]
-        R = [R[c][1:] - f * R[c][0:1] for c in range(2)]
+        R = R[1:] - f * R[0:1]
         F.append(f)
-    piv = jnp.concatenate([S[j][0:1] for j in range(BK)], 0)
-    rs = lax.rsqrt(piv)
-    U = [jnp.concatenate(out[c], 0) for c in range(2)]
-    for c in range(2):
-        v = U[c] * rs
-        if c == t:
-            v = jnp.where(lane < o + BK, v, 0.0)
-        elif c > t:
-            v = jnp.zeros_like(v)
-        for i in range(BK):
-            w_ref[k + i : k + i + 1, c * 128 : c * 128 + 128] = v[i, 0:1]
+    rs = lax.rsqrt(jnp.concatenate([S[j][0:1] for j in range(BK)], 0))
+    U = jnp.concatenate(out, 0)
+    v = jnp.where(at < BK, U * rs, 0.0)
+    for i in range(BK):
+        for c in range(2):
+            w_ref[k + i : k + i + 1, c * 128 : c * 128 + 128] = v[i, 4 * c : 4 * c + 1]
     if k + BK >= NB:
         return
-    iv = jnp.concatenate(inv, 0)
-    Z = [U[c] * iv for c in range(2)]
+    Z = U * jnp.concatenate(inv, 0)
     for i in reversed(range(BK)):
         for c in range(2):
-            g_ref[i : i + 1, c * 128 : c * 128 + 128] = Z[c][i, 0:1]
+            g_ref[i : i + 1, c * 128 : c * 128 + 128] = Z[i, 4 * c : 4 * c + 1]
         if i:
             f = jnp.concatenate([F[n][i - n - 1 : i - n] for n in range(i)], 0)
-            Z = [Z[c][:i] - f * Z[c][i : i + 1] for c in range(2)]
+            Z = Z[:i] - f * Z[i : i + 1]
     gh, gm, gl = split3(g_ref[...])
-    for q, (a, b) in enumerate(((gh, gh), (gm, gm), (gl, gh))):
-        rhs_ref[q, o : o + BK, :] = a
-        rhs_ref[q, 128 + o : 128 + o + BK, :] = b
+    for q, a in enumerate((gh, gh, gm, gm, gl, gh)):
+        rhs_ref[q * 128 + o : q * 128 + o + BK, :] = a
     n0 = k + BK
     h, m, l = split3(m_ref[n0:NB, t * 128 : t * 128 + 128])
-    hm = jnp.concatenate([h, m], 1)
-    up = dot(hm, rhs_ref[0]) + dot(hm, rhs_ref[1])
-    up = up + dot(jnp.concatenate([h, l], 1), rhs_ref[2])
+    up = dot(jnp.concatenate([h, m, h, m, h, l], 1), rhs_ref[...])
     lanes = lax.broadcasted_iota(jnp.int32, (NB - n0, NB), 1)
     old = jnp.where((lanes >= k) & (lanes < k + BK), 0.0, m_ref[n0:NB, :])
     m_ref[n0:NB, :] = old - up
     zero = jnp.zeros((BK, NB), bf16)
-    for q in range(3):
-        rhs_ref[q, o : o + BK, :] = zero
-        rhs_ref[q, 128 + o : 128 + o + BK, :] = zero
+    for q in range(6):
+        rhs_ref[q * 128 + o : q * 128 + o + BK, :] = zero
 
 
 class Torus:
@@ -110,12 +102,12 @@
         return jnp.where(same == 1, y, 3 - y) % 2, 1 - same
 
 
-NSEM = 37
+NSEM = 45
 
 
 class Share:
     def __init__(self, me, half, row_ref, col_ref, send, recv):
-        self.me = me
+        self.me, self.ring = me, half == 0
         self.row, self.col = row_ref.at[half], col_ref.at[half]
         self.send, self.recv = send.at[half], recv.at[half]
         self.started = []
@@ -150,12 +142,12 @@
         return self.row.at[2 * ((me.z + 4 - d) % 4) + (me.c + e) % 2]
 
     def second(self, part, e):
-        for d in range(1, 4):
+        for d in (1, 3) if self.ring else (2, 1, 3):
             self.go(self.chunk(part, e), 6 + 12 * part + 3 * e + d - 1, self.me.step("yx"[part], d))
 
     def begin(self):
         for part in range(2):
-            for d in range(1, 4):
+            for d in (2, 1, 3):
                 self.go(self.chunk(part), 3 * part + d - 1, self.me.step("xy"[part], d))
         for part in range(2):
             self.second(part, 0)
@@ -174,11 +166,26 @@
                 self.wait(self.chunk(part, e), 3 * part + e - 1)
                 self.second(part, e)
 
+    def far(self, part, e, which):
+        return self.chunk(part, e, 2).at[which * 48 : which * 48 + 48], (6 + 12 * part + 3 * e + 1, 37 + 4 * part + e)[which]
+
+    def forward(self):
+        for e in (0, 1, 3, 2):
+            for part in range(2):
+                for which, d in enumerate((1, 3)):
+                    whole = self.chunk(part, e, d)
+                    self.wait(whole, 6 + 12 * part + 3 * e + d - 1)
+                    self.go(whole.at[which * 48 : which * 48 + 48], self.far(part, e, which)[1], self.me.step("yx"[part], d))
+
     def finish(self):
         for i, (d, e) in enumerate(self.others()):
             self.wait(self.rowblock(d, e), 30 + i)
         for e in (0, 1, 3, 2):
             for part in range(2):
+                if self.ring:
+                    for which in range(2):
+                        self.wait(*self.far(part, e, which))
+                    continue
                 for d in range(1, 4):
                     self.wait(self.chunk(part, e, d), 6 + 12 * part + 3 * e + d - 1)
         for cp in self.started:
@@ -210,69 +217,43 @@
     a_hbm, b_hbm, v_hbm, t_hbm, r_hbm, panel_ref, white_ref, wh_ref, row_ref, col_ref, t_ref, r_ref,
     m_ref, w_ref, g_ref, rhs_ref, bv_ref, held_ref, send, recv, first, local,
 ):
-    loads = [
-        pltpu.make_async_copy(a_hbm, m_ref, local.at[0]),
-        pltpu.make_async_copy(b_hbm, bv_ref.at[0:RB], local.at[1]),
-        pltpu.make_async_copy(v_hbm, bv_ref.at[RB:NB], local.at[2]),
-    ]
-    for cp in loads:
-        cp.start()
     me = Torus()
     barrier, count = greet(me)
-    rhs_ref[...] = jnp.zeros_like(rhs_ref)
-    shares = [Share(me, h, row_ref, col_ref, send, recv) for h in range(2)]
     holder = me.at(me.z, jnp.where(me.c == 0, me.y, 3 - me.y), me.x, me.y // 2)
-    raw = []
-    for h in range(2):
-        src = b_hbm.at[:, h * 128 : h * 128 + 128]
-        raw.append(
+    halves = [b_hbm.at[:, h * 128 : h * 128 + 128] for h in range(2)]
+    spans = [w_ref.at[0:128, 0:128], w_ref.at[128:NB]]
+
+    def flow(lead):
+        loads = [
+            pltpu.make_async_copy(b_hbm, bv_ref.at[0:RB], local.at[1]),
+            pltpu.make_async_copy(v_hbm, bv_ref.at[RB:NB], local.at[2]),
+        ]
+        later = [pltpu.make_async_copy(t_hbm, t_ref, local.at[3]), pltpu.make_async_copy(r_hbm, r_ref, local.at[4])]
+        shares = [Share(me, h, row_ref, col_ref, send, recv) for h in range(2)]
+        raw = [
             pltpu.make_async_remote_copy(
-                src_ref=src,
+                src_ref=halves[h],
                 dst_ref=held_ref.at[h],
                 send_sem=first.at[2 + h],
                 recv_sem=first.at[h],
                 device_id=holder,
                 device_id_type=MESH,
             )
-        )
-    loads[0].wait()
-    later = [pltpu.make_async_copy(t_hbm, t_ref, local.at[3]), pltpu.make_async_copy(r_hbm, r_ref, local.at[4])]
-    for cp in later:
-        cp.start()
-
-    def solve(b, w):
-        n = b.shape[1]
-        bh, bm, _ = split3(b)
-        wh, wm, _ = split3(w)
-        return dot_nt(bh, wh) + (dot_nt(bh, wm) + dot_nt(bm, wh))
-
-    def part_of(half):
-        c0, n = half * 128, half * 128 + 128
-        w = w_ref[c0:n, 0:n]
-        raw[half].wait_recv()
-        if half == 0:
-            b = held_ref[0]
-        else:
-            b = jnp.concatenate([held_ref[0], held_ref[1]], 1)
-        xb = solve(b, w).astype(bf16)
-        for part in range(2):
-            shares[half].chunk(part)[...] = xb[part * 96 : part * 96 + 96]
-        if half == 0:
-            loads[1].wait()
-            loads[2].wait()
-        x = solve(bv_ref[:, 0:n], w)
-        xb = x.astype(bf16)
-        for part in range(2):
-            row_ref[half, 2 * me.z + me.c, part] = xb[part * 96 : part * 96 + 96]
-        shares[half].begin()
-        panel_ref[:, c0:n] = x[0:RB]
-        white_ref[:, c0:n] = x[RB:NB]
-        wh_ref[:, c0:n] = xb[RB:NB]
-        shares[half].rows()
-
-    for i in range(NB // BK):
-        block_step(i * BK, m_ref, w_ref, g_ref, rhs_ref)
-        if i == 0:
+            for h in range(2)
+        ]
+        gift = [
+            pltpu.make_async_remote_copy(
+                src_ref=spans[h],
+                dst_ref=spans[h],
+                send_sem=first.at[6 + h],
+                recv_sem=first.at[4 + h],
+                device_id=me.at(c=1 - me.c),
+                device_id_type=MESH,
+            )
+            for h in range(2)
+        ]
+
+        def enter():
             pl.semaphore_wait(barrier, count)
 
             @pl.when(me.other)
@@ -283,24 +264,87 @@
             @pl.when(me.own)
             def _():
                 for h in range(2):
-                    pltpu.make_async_copy(b_hbm.at[:, h * 128 : h * 128 + 128], held_ref.at[h], first.at[h]).start()
-
-        if i == SEND_AFTER:
+                    pltpu.make_async_copy(halves[h], held_ref.at[h], first.at[h]).start()
+
+        def solve(b, w):
+            bh, bm, _ = split3(b)
+            wh, wm, _ = split3(w)
+            return dot_nt(bh, wh) + (dot_nt(bh, wm) + dot_nt(bm, wh))
+
+        def part_of(half):
+            c0, n = half * 128, half * 128 + 128
+            raw[half].wait_recv()
+            if not lead:
+                gift[half].wait_recv()
+            w = w_ref[c0:n, 0:n]
+            if half == 0:
+                b = held_ref[0]
+            else:
+                b = jnp.concatenate([held_ref[0], held_ref[1]], 1)
+            xb = solve(b, w).astype(bf16)
+            for part in range(2):
+                shares[half].chunk(part)[...] = xb[part * 96 : part * 96 + 96]
+            if lead and half == 1:
+                gift[1].start()
+            if half == 0:
+                for cp in loads:
+                    cp.wait()
+            x = solve(bv_ref[:, 0:n], w)
+            xb = x.astype(bf16)
+            for part in range(2):
+                row_ref[half, 2 * me.z + me.c, part] = xb[part * 96 : part * 96 + 96]
+            shares[half].begin()
+            panel_ref[:, c0:n] = x[0:RB]
+            white_ref[:, c0:n] = x[RB:NB]
+            wh_ref[:, c0:n] = xb[RB:NB]
+            shares[half].rows()
+
+        if lead:
+            diag = pltpu.make_async_copy(a_hbm, m_ref, local.at[0])
+            diag.start()
+            for cp in loads:
+                cp.start()
+            rhs_ref[...] = jnp.zeros_like(rhs_ref)
+            diag.wait()
+            for cp in later:
+                cp.start()
+            for i in range(NB // BK):
+                block_step(i * BK, m_ref, w_ref, g_ref, rhs_ref)
+                if i == 0:
+                    enter()
+                if i == 8:
+                    gift[0].start()
+                if i == SEND_AFTER:
+                    part_of(0)
+                if i == RELAY_AFTER:
+                    shares[0].relay()
+        else:
+            enter()
+            for cp in loads + later:
+                cp.start()
             part_of(0)
-        if i == RELAY_AFTER:
             shares[0].relay()
-    part_of(1)
-    shares[1].relay()
-    for s in shares:
-        s.finish()
-
-    @pl.when(me.other)
-    def _():
-        for cp in raw:
-            cp.wait_send()
-
-    for cp in later:
-        cp.wait()
+        part_of(1)
+        if lead and RELAY_AFTER > 15:
+            shares[0].relay()
+        shares[0].forward()
+        shares[1].relay()
+        for s in shares:
+            s.finish()
+        if lead:
+            for cp in gift:
+                cp.wait_send()
+
+        @pl.when(me.other)
+        def _():
+            for cp in raw:
+                cp.wait_send()
+
+        for cp in later:
+            cp.wait()
+
+    pl.when(me.c == 0)(lambda: flow(True))
+    pl.when(me.c == 1)(lambda: flow(False))
 
 
 def update_kernel(row_ref, col_ref, t_ref, wh_ref, v_ref, p_in, w_in, out_ref, vec_ref, p_ref, w_ref):
@@ -321,7 +365,7 @@
 
 VM = pl.BlockSpec(memory_space=pltpu.VMEM)
 HB = pl.BlockSpec(memory_space=pltpu.MemorySpace.HBM)
-SEND_AFTER, RELAY_AFTER = 9, 14
+SEND_AFTER, RELAY_AFTER = 14, 16
 
 
 def per_device(diag_tile, panel_block, trailing, vec_head, vec_rest):
@@ -348,12 +392,12 @@
             pltpu.VMEM((NB, NB), f32),
             pltpu.VMEM((NB, NB), f32),
             pltpu.VMEM((BK, NB), f32),
-            pltpu.VMEM((3, NB, NB), bf16),
+            pltpu.VMEM((3 * NB, NB), bf16),
             pltpu.VMEM((NB, NB), f32),
             pltpu.VMEM((2, RB, 128), f32),
             pltpu.SemaphoreType.DMA((2, NSEM)),
             pltpu.SemaphoreType.DMA((2, NSEM)),
-            pltpu.SemaphoreType.DMA((4,)),
+            pltpu.SemaphoreType.DMA((8,)),
             pltpu.SemaphoreType.DMA((5,)),
         ],
         compiler_params=pltpu.CompilerParams(

time: 42.4 us -> 40.6 us (0.958)
  Pallas kernels: 41.3 us -> 39.8 us
    pallas_call x1, Pallas kernels: 35.5 us -> 34.1 us  [per_device(): pl.pallas_call(panel_kernel, out_shape=(jax.ShapeDtypeStruct((RB, NB), f3...]
where the time goes in v4:
time: 40.6 us; the launch traced here: 40.5 us
  Pallas kernels  39.8 us (98%)
  between operations  0.64 us (2%)
    pallas_call x1, Pallas kernels, per_device(): pl.pallas_call(panel_kernel, out_shape=(jax.ShapeDtypeStruct((RB, NB), f3...  34.1 us
    pallas_call x1, Pallas kernels, per_device(): pl.pallas_call(update_kernel, grid=(mr // tm,), out_shape=(jax.ShapeDtype...  5.78 us

profile of v4, /device:TPU:0, one launch (start us, length us, event | category | flops | bytes accessed | tf_op | source)
XLA Modules:
  0.0 40.5 jit_solution(11865890800687985409)
XLA Ops:
  0.6 34.1 %panel.1 = (f32[192,256]{1,0:T(8,128)S(1)}, f32[64,256]{1,0:T(8,128)S(1)}, bf16[64,256]{1,0:T(8,128)(2,1)S(1)}, bf16[2,8,2,96,128]{4,3,2,1,0:T(8,128)(2,1)S(1)},...) custom-call(f32[256,256]{1,0:T(8,128)} %a_hbm.1, ...), custom_call_target="tpu_custom_call" | custom-call | flops 20000000000 | tf_op jit(solution)/shard_map/panel/pallas_call | solution.py:378
  34.7 5.8 %update.1 = (bf16[1536,3072]{1,0:T(8,128)(2,1)}, f32[64,1536]{1,0:T(8,128)}, f32[192,256]{1,0:T(8,128)}, f32[64,256]{1,0:T(8,128)}) custom-call(bf16[2,1536,128]{2,1,0:T(8,128)(2,1)S(1)} %bitcast.3, bf16[2,3072,128]{2,1,0:T(8,128)(2,1)S(1)} %bitcast.2, bf16[1536,3072]{1,0:T(8,128)(2,1)S(1)} %get-tuple-element.17.t_ref, ...), custom_call_target="tpu_custom_call" | custom-call | tf_op jit(solution)/shard_map/update/pallas_call | solution.py:413

commit v5 on v4

--- a/solution.py
+++ b/solution.py
@@ -107,7 +107,7 @@
 
 class Share:
     def __init__(self, me, half, row_ref, col_ref, send, recv):
-        self.me, self.ring = me, half == 0
+        self.me, self.ring, self.diag = me, half == 0, DIAG[half]
         self.row, self.col = row_ref.at[half], col_ref.at[half]
         self.send, self.recv = send.at[half], recv.at[half]
         self.started = []
@@ -141,7 +141,18 @@
         me = self.me
         return self.row.at[2 * ((me.z + 4 - d) % 4) + (me.c + e) % 2]
 
+    def across(self, part):
+        dims = "xy" if part == 0 else "yx"
+        for e in (1, 3):
+            for d in (1, 3):
+                to = {dims[0]: (getattr(self.me, dims[0]) + e) % 4, dims[1]: (getattr(self.me, dims[1]) + d) % 4}
+                self.go(self.chunk(part), 6 + 12 * part + 3 * e + d - 1, self.me.at(**to))
+
     def second(self, part, e):
+        if self.diag and e in (1, 3):
+            if not self.ring:
+                self.go(self.chunk(part, e), 6 + 12 * part + 3 * e + 1, self.me.step("yx"[part], 2))
+            return
         for d in (1, 3) if self.ring else (2, 1, 3):
             self.go(self.chunk(part, e), 6 + 12 * part + 3 * e + d - 1, self.me.step("yx"[part], d))
 
@@ -151,6 +162,9 @@
                 self.go(self.chunk(part), 3 * part + d - 1, self.me.step("xy"[part], d))
         for part in range(2):
             self.second(part, 0)
+        if self.diag:
+            for part in range(2):
+                self.across(part)
 
     def others(self):
         return [(d, e) for d in range(4) for e in range(2) if d or e]
@@ -210,7 +224,10 @@
     for dim in "xy":
         for d in range(1, 4):
             tell(me.step(dim, d))
-    return barrier, 14 - jnp.where(me.own, 1, 0)
+    for e in (1, 3):
+        for d in (1, 3):
+            tell(me.at(x=(me.x + e) % 4, y=(me.y + d) % 4))
+    return barrier, 18 - jnp.where(me.own, 1, 0)
 
 
 def panel_kernel(
@@ -365,7 +382,8 @@
 
 VM = pl.BlockSpec(memory_space=pltpu.VMEM)
 HB = pl.BlockSpec(memory_space=pltpu.MemorySpace.HBM)
-SEND_AFTER, RELAY_AFTER = 14, 16
+SEND_AFTER, RELAY_AFTER = 13, 16
+DIAG = (True, False)
 
 
 def per_device(diag_tile, panel_block, trailing, vec_head, vec_rest):

time: 40.6 us -> 40.3 us (level)
  no operation moved by 1% of the time
where the time goes in v5:
time: 40.3 us; the launch traced here: 40.2 us
  Pallas kernels  39.5 us (98%)
  between operations  0.64 us (2%)
    pallas_call x1, Pallas kernels, per_device(): pl.pallas_call(panel_kernel, out_shape=(jax.ShapeDtypeStruct((RB, NB), f3...  33.8 us
    pallas_call x1, Pallas kernels, per_device(): pl.pallas_call(update_kernel, grid=(mr // tm,), out_shape=(jax.ShapeDtype...  5.77 us

profile of v5, /device:TPU:0, one launch (start us, length us, event | category | flops | bytes accessed | tf_op | source)
XLA Modules:
  0.0 40.2 jit_solution(6606538587875386690)
XLA Ops:
  0.6 33.8 %panel.1 = (f32[192,256]{1,0:T(8,128)S(1)}, f32[64,256]{1,0:T(8,128)S(1)}, bf16[64,256]{1,0:T(8,128)(2,1)S(1)}, bf16[2,8,2,96,128]{4,3,2,1,0:T(8,128)(2,1)S(1)},...) custom-call(f32[256,256]{1,0:T(8,128)} %a_hbm.1, ...), custom_call_target="tpu_custom_call" | custom-call | flops 20000000000 | tf_op jit(solution)/shard_map/panel/pallas_call | solution.py:396
  34.4 5.8 %update.1 = (bf16[1536,3072]{1,0:T(8,128)(2,1)}, f32[64,1536]{1,0:T(8,128)}, f32[192,256]{1,0:T(8,128)}, f32[64,256]{1,0:T(8,128)}) custom-call(bf16[2,1536,128]{2,1,0:T(8,128)(2,1)S(1)} %bitcast.3, bf16[2,3072,128]{2,1,0:T(8,128)(2,1)S(1)} %bitcast.2, bf16[1536,3072]{1,0:T(8,128)(2,1)S(1)} %get-tuple-element.17.t_ref, ...), custom_call_target="tpu_custom_call" | custom-call | tf_op jit(solution)/shard_map/update/pallas_call | solution.py:431
